TPU v7x, 768 devices: a whole 4x8x12 slice. The times are simulated.
768 devices in a mesh: row: 16 (over x, y_hi, core), col: 48 (over y_lo, z).
Axes of the slice: x: 4, y: 8 (y_hi: 2, y_lo: 4; y = y_hi * 4 + y_lo), z: 12, core: 2. Of those that a mesh axis runs over, the one named last changes fastest.
Arguments:
- vectors: bfloat16 [16, 196608], P(None, ('row', 'col')), may hold values from -6 to 6
- tiles: bfloat16 [98304, 128, 128], P(('row', 'col')), may hold values from -0.046875 to 0.046875
- tile_rows: int32 [98304], P(('row', 'col')), may hold values from 0 to 95
- tile_cols: int32 [98304], P(('row', 'col')), may hold values from 0 to 95
- tile_count: int32 [768], P(('row', 'col')), may hold values from 32 to 128, as said below
Outputs:
- applied: float32 [16, 196608], P(None, ('row', 'col'))
Inputs may be any that keep to these rules, and one draw needn't show every extreme that they name: `tile_count`: each device has between 32 and 128 live slots; some device fills all 128.
All inputs are finite; a program needn't handle non-finite values.
Results may differ from a plain program's by a relative error of at most 0.0003.
Values may be sent and summed in bfloat16 or wider, within the bound.
No kernel may reach another device: no remote copies, remote signals or barrier semaphores. Data moves between devices by JAX's collectives and lax.ppermute only.
A program may use at most 32 MiB of HBM per device.

v0:
```python
import functools

import jax
import jax.numpy as jnp
from jax import lax
from jax.experimental import pallas as pl
from jax.experimental.pallas import tpu as pltpu
from jax.sharding import PartitionSpec as P

CHUNK = 16
GROUP = 8
TOP = 14
TAKERS_OUT = (
    (8, 5, 4, 27, 20, 31, 34, 47, 46, 39, 38, 9, 12, 1, 24, 25, 28, 21, 16, 35, 44, 33, 0, 13, 6, 7, 18, 29, 30, 17, 32, 41, 40, 37, 36, 11, 10, 15, 14, 19, 22, 23, 26, 43, 42, 45, 2, 3),
    (8, 13, 0, 1, 16, 25, 30, 35, 38, 47, 42, 5, 4, 9, 12, 17, 24, 29, 28, 21, 36, 43, 34, 33, 2, 15, 6, 7, 20, 23, 26, 37, 44, 45, 40, 41, 14, 11, 10, 31, 18, 27, 22, 19, 32, 39, 46, 3),
    (6, 11, 10, 7, 2, 25, 28, 17, 40, 41, 44, 37, 32, 15, 14, 3, 22, 27, 26, 23, 30, 33, 36, 39, 34, 9, 0, 1, 18, 19, 24, 31, 46, 43, 42, 47, 12, 13, 8, 5, 4, 21, 20, 29, 16, 45, 38, 35),
    (44, 3, 10, 11, 6, 7, 18, 27, 20, 33, 40, 41, 42, 39, 2, 15, 14, 19, 30, 31, 26, 23, 34, 45, 38, 47, 4, 5, 8, 1, 16, 25, 22, 35, 46, 43, 32, 9, 0, 13, 12, 29, 28, 21, 24, 17, 36, 37),
    (46, 43, 8, 13, 12, 5, 4, 23, 18, 19, 42, 47, 34, 39, 38, 1, 0, 9, 16, 17, 28, 29, 24, 35, 40, 41, 44, 11, 10, 3, 20, 21, 22, 25, 36, 37, 32, 33, 6, 7, 14, 15, 2, 31, 30, 27, 26, 45),
    (38, 47, 46, 35, 12, 13, 8, 9, 26, 27, 30, 39, 42, 43, 34, 5, 4, 1, 0, 25, 24, 17, 28, 29, 44, 37, 36, 3, 6, 11, 2, 7, 16, 19, 20, 21, 40, 45, 32, 41, 10, 15, 14, 23, 22, 31, 18, 33),
    (36, 45, 44, 33, 32, 15, 14, 3, 10, 23, 26, 19, 22, 41, 40, 37, 6, 7, 2, 11, 18, 31, 30, 27, 34, 35, 46, 39, 38, 5, 8, 1, 4, 21, 16, 17, 24, 47, 42, 43, 0, 9, 12, 13, 20, 25, 28, 29),
    (24, 33, 32, 45, 44, 37, 10, 15, 2, 7, 16, 29, 30, 31, 36, 41, 40, 11, 6, 3, 14, 27, 18, 19, 26, 39, 38, 43, 46, 47, 4, 5, 0, 1, 22, 23, 20, 21, 34, 35, 42, 9, 8, 13, 12, 17, 28, 25),
    (18, 19, 26, 35, 38, 39, 34, 1, 0, 5, 4, 23, 22, 21, 42, 47, 46, 43, 12, 9, 8, 13, 24, 25, 16, 17, 20, 37, 44, 41, 40, 15, 14, 7, 28, 29, 30, 27, 36, 33, 32, 45, 6, 11, 2, 3, 10, 31),
    (26, 23, 18, 39, 34, 35, 46, 43, 0, 1, 12, 27, 28, 31, 24, 25, 42, 47, 38, 13, 4, 5, 8, 9, 20, 17, 16, 29, 32, 45, 36, 33, 10, 15, 6, 21, 22, 19, 30, 41, 40, 37, 44, 3, 2, 11, 14, 7),
    (16, 29, 24, 25, 20, 33, 40, 41, 44, 3, 6, 7, 10, 21, 22, 27, 36, 45, 32, 37, 14, 11, 2, 15, 30, 31, 18, 19, 26, 43, 38, 39, 46, 9, 8, 13, 4, 17, 28, 23, 42, 47, 34, 35, 12, 5, 0, 1),
    (2, 11, 20, 21, 24, 25, 32, 33, 40, 41, 14, 15, 6, 3, 28, 29, 30, 23, 44, 45, 36, 37, 10, 7, 12, 27, 22, 19, 18, 31, 46, 47, 42, 43, 8, 9, 0, 1, 26, 17, 16, 35, 38, 39, 34, 13, 4, 5),
    (14, 9, 30, 23, 26, 19, 42, 43, 46, 47, 38, 11, 0, 1, 12, 27, 22, 29, 20, 39, 34, 35, 4, 5, 8, 13, 28, 17, 24, 25, 16, 41, 32, 33, 44, 15, 10, 3, 2, 21, 18, 31, 40, 37, 36, 45, 6, 7),
    (12, 3, 6, 31, 18, 27, 22, 47, 38, 43, 34, 35, 8, 5, 4, 1, 30, 23, 26, 29, 42, 39, 46, 13, 0, 9, 10, 25, 16, 21, 20, 17, 44, 41, 32, 33, 2, 7, 14, 15, 24, 19, 28, 45, 40, 37, 36, 11),
    (40, 1, 0, 11, 28, 21, 20, 29, 32, 37, 36, 33, 6, 3, 2, 7, 10, 27, 24, 31, 30, 45, 44, 41, 14, 13, 8, 15, 26, 19, 22, 23, 18, 39, 38, 47, 42, 5, 4, 9, 12, 17, 16, 25, 46, 43, 34, 35),
    (36, 41, 10, 1, 0, 29, 20, 21, 28, 45, 32, 37, 44, 11, 6, 7, 2, 3, 30, 25, 16, 27, 40, 33, 38, 15, 14, 9, 4, 23, 18, 19, 22, 31, 46, 39, 34, 47, 12, 5, 8, 13, 26, 17, 24, 35, 42, 43),
)
TAKERS_BACK = (
    (8, 5, 4, 27, 20, 31, 34, 47, 46, 39, 38, 9, 12, 1, 24, 25, 28, 21, 16, 35, 44, 33, 0, 13, 6, 7, 18, 29, 30, 17, 32, 41, 40, 37, 36, 11, 10, 15, 14, 19, 22, 23, 26, 43, 42, 45, 2, 3),
    (8, 13, 0, 1, 16, 25, 30, 35, 38, 47, 42, 5, 4, 9, 12, 17, 24, 29, 28, 21, 36, 43, 34, 33, 2, 15, 6, 7, 20, 23, 26, 37, 44, 45, 40, 41, 14, 11, 10, 31, 18, 27, 22, 19, 32, 39, 46, 3),
    (6, 11, 10, 7, 2, 25, 28, 17, 40, 41, 44, 37, 32, 15, 14, 3, 22, 27, 26, 23, 30, 33, 36, 39, 34, 9, 0, 1, 18, 19, 24, 31, 46, 43, 42, 47, 12, 13, 8, 5, 4, 21, 20, 29, 16, 45, 38, 35),
    (44, 3, 10, 11, 6, 7, 18, 27, 20, 33, 40, 41, 42, 39, 2, 15, 14, 19, 30, 31, 26, 23, 34, 45, 38, 47, 4, 5, 8, 1, 16, 25, 22, 35, 46, 43, 32, 9, 0, 13, 12, 29, 28, 21, 24, 17, 36, 37),
    (46, 43, 8, 13, 12, 5, 4, 23, 18, 19, 42, 47, 34, 39, 38, 1, 0, 9, 16, 17, 28, 29, 24, 35, 40, 41, 44, 11, 10, 3, 20, 21, 22, 25, 36, 37, 32, 33, 6, 7, 14, 15, 2, 31, 30, 27, 26, 45),
    (38, 47, 46, 35, 12, 13, 8, 9, 26, 27, 30, 39, 42, 43, 34, 5, 4, 1, 0, 25, 24, 17, 28, 29, 44, 37, 36, 3, 6, 11, 2, 7, 16, 19, 20, 21, 40, 45, 32, 41, 10, 15, 14, 23, 22, 31, 18, 33),
    (36, 45, 44, 33, 32, 15, 14, 3, 10, 23, 26, 19, 22, 41, 40, 37, 6, 7, 2, 11, 18, 31, 30, 27, 34, 35, 46, 39, 38, 5, 8, 1, 4, 21, 16, 17, 24, 47, 42, 43, 0, 9, 12, 13, 20, 25, 28, 29),
    (24, 33, 32, 45, 44, 37, 10, 15, 2, 7, 16, 29, 30, 31, 36, 41, 40, 11, 6, 3, 14, 27, 18, 19, 26, 39, 38, 43, 46, 47, 4, 5, 0, 1, 22, 23, 20, 21, 34, 35, 42, 9, 8, 13, 12, 17, 28, 25),
    (18, 19, 26, 35, 38, 39, 34, 1, 0, 5, 4, 23, 22, 21, 42, 47, 46, 43, 12, 9, 8, 13, 24, 25, 16, 17, 20, 37, 44, 41, 40, 15, 14, 7, 28, 29, 30, 27, 36, 33, 32, 45, 6, 11, 2, 3, 10, 31),
    (26, 23, 18, 39, 34, 35, 46, 43, 0, 1, 12, 27, 28, 31, 24, 25, 42, 47, 38, 13, 4, 5, 8, 9, 20, 17, 16, 29, 32, 45, 36, 33, 10, 15, 6, 21, 22, 19, 30, 41, 40, 37, 44, 3, 2, 11, 14, 7),
    (16, 29, 24, 25, 20, 33, 40, 41, 44, 3, 6, 7, 10, 21, 22, 27, 36, 45, 32, 37, 14, 11, 2, 15, 30, 31, 18, 19, 26, 43, 38, 39, 46, 9, 8, 13, 4, 17, 28, 23, 42, 47, 34, 35, 12, 5, 0, 1),
    (2, 11, 20, 21, 24, 25, 32, 33, 40, 41, 14, 15, 6, 3, 28, 29, 30, 23, 44, 45, 36, 37, 10, 7, 12, 27, 22, 19, 18, 31, 46, 47, 42, 43, 8, 9, 0, 1, 26, 17, 16, 35, 38, 39, 34, 13, 4, 5),
    (14, 9, 30, 23, 26, 19, 42, 43, 46, 47, 38, 11, 0, 1, 12, 27, 22, 29, 20, 39, 34, 35, 4, 5, 8, 13, 28, 17, 24, 25, 16, 41, 32, 33, 44, 15, 10, 3, 2, 21, 18, 31, 40, 37, 36, 45, 6, 7),
    (12, 3, 6, 31, 18, 27, 22, 47, 38, 43, 34, 35, 8, 5, 4, 1, 30, 23, 26, 29, 42, 39, 46, 13, 0, 9, 10, 25, 16, 21, 20, 17, 44, 41, 32, 33, 2, 7, 14, 15, 24, 19, 28, 45, 40, 37, 36, 11),
    (40, 1, 0, 11, 28, 21, 20, 29, 32, 37, 36, 33, 6, 3, 2, 7, 10, 27, 24, 31, 30, 45, 44, 41, 14, 13, 8, 15, 26, 19, 22, 23, 18, 39, 38, 47, 42, 5, 4, 9, 12, 17, 16, 25, 46, 43, 34, 35),
    (36, 41, 10, 1, 0, 29, 20, 21, 28, 45, 32, 37, 44, 11, 6, 7, 2, 3, 30, 25, 16, 27, 40, 33, 38, 15, 14, 9, 4, 23, 18, 19, 22, 31, 46, 39, 34, 47, 12, 5, 8, 13, 26, 17, 24, 35, 42, 43),
)


def grant(mib):
    return pltpu.CompilerParams(vmem_limit_bytes=mib * 2**20)


def vmem():
    return pl.BlockSpec(memory_space=pltpu.VMEM)


def powers(exponent):
    low = exponent >> 1
    return (
        jnp.exp2(low.astype(jnp.float32)),
        jnp.exp2((exponent - low).astype(jnp.float32)),
    )


def pack(sums, payload, at):
    group, _, rows, width = sums.shape
    half = rows // 2
    peak = jnp.max(jnp.max(jnp.abs(sums), axis=1), axis=-1, keepdims=True)
    peak = jnp.maximum(peak, 1.2e-38)
    exponent = jnp.floor(jnp.log2(peak)).astype(jnp.int32)
    first, second = powers(TOP - exponent)
    for s in range(2):
        scaled = jnp.round((sums[:, s] * first) * second)
        scaled = jnp.minimum(jnp.maximum(scaled, -32767.0), 32767.0)
        scaled = scaled.astype(jnp.int32).astype(jnp.int16)
        payload[pl.ds(at, group), s * rows : (s + 1) * rows] = scaled
    lane = lax.broadcasted_iota(jnp.int32, (group, half, width), 2)
    both = jnp.where(lane < width // 2, exponent[:, :half], exponent[:, half:])
    payload[pl.ds(at, group), 2 * rows : 2 * rows + half] = both.astype(jnp.int16)


def unpack(payload, at, group, rows):
    half = rows // 2
    width = payload.shape[-1]
    exponent = payload[pl.ds(at, group), 2 * rows : 2 * rows + half].astype(jnp.int32)
    factors = []
    for factor in powers(exponent - TOP):
        upper = jnp.broadcast_to(factor[:, :, :1], (group, half, width))
        lower = factor[:, :, width // 2 : width // 2 + 1]
        lower = jnp.broadcast_to(lower, (group, half, width))
        factors.append(jnp.concatenate([upper, lower], axis=1))
    parts = [payload[pl.ds(at, group), s * rows : (s + 1) * rows] for s in range(2)]
    return [(part.astype(jnp.float32) * factors[0]) * factors[1] for part in parts]


def product_kernel(mirror, meta, sources, targets, *refs):
    if mirror:
        own, tiles, keep, give, x, held, sems, acc = refs
        parts = [own]
    else:
        mine, theirs, held, acc, x = refs
        parts = [mine, theirs]
    width = held.shape[1]
    chunks = held.shape[0] // CHUNK

    def copy(step):
        part = pl.ds(step * CHUNK, CHUNK)
        return pltpu.make_async_copy(tiles.at[part], held.at[part], sems.at[step])

    if mirror:
        for step in range(chunks):
            copy(step).start()
    at = 0
    for part in parts:
        size = part.shape[0]
        for s in range(2):
            x[at : at + size, s] = part[:, :, s * width : (s + 1) * width]
        at += size
    x[at] = jnp.zeros(x.shape[1:], x.dtype)
    acc[...] = jnp.zeros_like(acc)

    def step_body(step, carry):
        if mirror:
            copy(step).wait()

        @pl.when(step * CHUNK < meta[0])
        def _():
            found = []
            for u in range(CHUNK):
                k = step * CHUNK + u
                source = sources[k]
                found.append(
                    lax.dot_general(
                        x[source // 2, source % 2],
                        held[k],
                        (((1,), (0 if mirror else 1,)), ((), ())),
                        preferred_element_type=jnp.float32,
                    )
                )
            for u in range(CHUNK):
                target = targets[step * CHUNK + u]
                acc[target // 2, target % 2] += found[u]

        return carry

    lax.fori_loop(0, chunks, step_body, 0)
    if mirror:
        half = keep.shape[0]
        keep[...] = acc[:half]
        give[...] = acc[half:]


def products(mirror, meta, sources, targets, segment, tiles):
    smem = pl.BlockSpec(memory_space=pltpu.SMEM)
    space = pltpu.HBM if mirror else pltpu.VMEM
    tiles = pltpu.with_memory_space_constraint(tiles, space)
    pieces = segment[0].shape[0] * len(segment)
    vecs = segment[0].shape[1]
    width = tiles.shape[1]
    scratch = [pltpu.VMEM((pieces + 1, 2, vecs, width), jnp.bfloat16)]
    if mirror:
        shapes = [jax.ShapeDtypeStruct((pieces // 2, 2, vecs, width), jnp.float32)] * 2
        outs = [vmem(), vmem()]
        scratch += [
            pltpu.VMEM(tiles.shape, tiles.dtype),
            pltpu.SemaphoreType.DMA((tiles.shape[0] // CHUNK,)),
            pltpu.VMEM((pieces, 2, vecs, width), jnp.float32),
        ]
    else:
        shapes = jax.ShapeDtypeStruct((pieces, 2, vecs, width), jnp.float32)
        outs = vmem()
    return pl.pallas_call(
        functools.partial(product_kernel, mirror),
        out_shape=shapes,
        in_specs=[smem] * 3 + [vmem()] * len(segment) + [pl.BlockSpec(memory_space=space)],
        out_specs=outs,
        scratch_shapes=scratch,
        compiler_params=grant(12 if mirror else 4),
    )(meta, sources, targets, *segment, tiles)


def join_kernel(keep, came, payload):
    def body(i, carry):
        part = pl.ds(i * GROUP, GROUP)
        pack(keep[part] + came[part], payload, i * GROUP)
        return carry

    lax.fori_loop(0, payload.shape[0] // GROUP, body, 0)


def join(keep, came):
    pieces, _, vecs, width = keep.shape
    return pl.pallas_call(
        join_kernel,
        out_shape=jax.ShapeDtypeStruct((pieces, 5 * vecs // 2, width), jnp.int16),
        in_specs=[vmem()] * 2,
        out_specs=vmem(),
        compiler_params=grant(4),
    )(keep, came)


def merge_kernel(side, sums, came, payload):
    pieces, _, vecs, _ = sums.shape
    half = pieces // 2
    first, other = side[0] * half, (1 - side[0]) * half

    def body(i, carry):
        at = i * GROUP
        added = jnp.stack(unpack(came, at, GROUP, vecs), axis=1)
        pack(sums[pl.ds(first + at, GROUP)] + added, payload, first + at)
        pack(sums[pl.ds(other + at, GROUP)], payload, other + at)
        return carry

    lax.fori_loop(0, half // GROUP, body, 0)


def merge(side, sums, came):
    pieces, _, vecs, width = sums.shape
    return pl.pallas_call(
        merge_kernel,
        out_shape=jax.ShapeDtypeStruct((pieces, 5 * vecs // 2, width), jnp.int16),
        in_specs=[pl.BlockSpec(memory_space=pltpu.SMEM)] + [vmem()] * 2,
        out_specs=vmem(),
        compiler_params=grant(4),
    )(side, sums, came)


def total_kernel(vecs, payload, out):
    width = payload.shape[-1]

    def body(i, sums):
        parts = unpack(payload, i * GROUP, GROUP, vecs)
        return tuple(one + part.sum(axis=0) for one, part in zip(sums, parts))

    zero = jnp.zeros((vecs, width), jnp.float32)
    sums = lax.fori_loop(0, payload.shape[0] // GROUP, body, (zero, zero))
    for s in range(2):
        out[:, s * width : (s + 1) * width] = sums[s]


def total(vecs, payload):
    return pl.pallas_call(
        functools.partial(total_kernel, vecs),
        out_shape=jax.ShapeDtypeStruct((vecs, 2 * payload.shape[-1]), jnp.float32),
        in_specs=[vmem()],
        out_specs=vmem(),
        compiler_params=grant(4),
    )(payload)


def handing(table, n_row, n_col):
    pairs = []
    for m in range(n_row):
        takers = [(r, c) for c in range(m, n_col, n_row) for r in range(n_row)]
        for c, taker in enumerate(table[m]):
            r, col = takers[taker]
            pairs.append((m * n_col + c, r * n_col + col))
    return pairs


def copies_kernel(array, out, sems):
    copies = [
        pltpu.make_async_copy(array, out.at[i], sems.at[i]) for i in range(out.shape[0])
    ]
    for copy in copies:
        copy.start()
    for copy in copies:
        copy.wait()


def spread(array, axes):
    size = lax.axis_size(axes)
    hbm = pl.BlockSpec(memory_space=pltpu.HBM)
    copies = pl.pallas_call(
        copies_kernel,
        out_shape=jax.ShapeDtypeStruct((size, *array.shape), array.dtype),
        in_specs=[hbm],
        out_specs=hbm,
        scratch_shapes=[pltpu.SemaphoreType.DMA((size,))],
        compiler_params=grant(2),
    )(pltpu.with_memory_space_constraint(array, pltpu.HBM))
    return lax.all_to_all(copies, axes, 0, 0, tiled=True)


def shards(out, back, vectors, tiles, tile_rows, tile_cols, tile_count):
    axes = ("row", "col")
    n_row, n_col = lax.axis_size("row"), lax.axis_size("col")
    vecs, slots = vectors.shape[0], tiles.shape[0]
    pieces = n_col // 2
    row_index, col_index = lax.axis_index("row"), lax.axis_index("col")
    core, side = row_index % 2, col_index % 2
    swap = [(r, r ^ 1) for r in range(n_row)]

    col_place = ((tile_cols // n_col) ^ core) * n_col + tile_cols % n_col
    nothing = 2 * n_col
    live = jnp.arange(slots, dtype=jnp.int32) < tile_count[0]
    mirrored = live & ((row_index != col_index % n_row) | (tile_rows != tile_cols))
    mirror_source = jnp.where(mirrored, tile_rows, nothing)
    plain_source = jnp.where(live, col_place, nothing)

    own = spread(vectors, "col")
    mine = lax.dynamic_slice_in_dim(own, side * pieces, pieces, 0)
    mine = lax.ppermute(mine, axes, out)
    keep, give = products(True, tile_count, mirror_source, col_place, [own], tiles)
    came = lax.ppermute(give, "row", swap)
    sums = join(keep, came)
    sums = lax.ppermute(sums, axes, back)

    theirs = lax.ppermute(mine, "row", swap)
    plain = products(False, tile_count, plain_source, tile_rows, [mine, theirs], tiles)
    plain = merge(side[None].astype(jnp.int32), plain, sums)
    plain = lax.all_to_all(plain, "col", 0, 0, tiled=True)
    return total(vecs, plain)


def solution(mesh):
    sizes = mesh.shape["row"], mesh.shape["col"]
    out = handing(TAKERS_OUT, *sizes)
    back = [(taker, giver) for giver, taker in handing(TAKERS_BACK, *sizes)]

    def step(*args):
        return shards(out, back, *args)

    both = ("row", "col")
    return jax.shard_map(
        step,
        mesh=mesh,
        in_specs=(P(None, both), P(both, None, None), P(both), P(both), P(both)),
        out_specs=P(None, both),
        check_vma=False,
    )
```

profile of v0, /device:TPU:6, one launch (start us, length us, event | category | flops | bytes accessed | tf_op | source)
XLA Modules:
  0.0 130.5 jit_solution(6991919813221354970)
XLA Ops:
  0.0 0.0 copy-start.1
  0.0 13.5 %shard_map.55 = bf16[48,16,256]{2,1,0:T(8,128)(2,1)} custom-call(bf16[16,256]{1,0:T(8,128)(2,1)} %array.1), custom_call_target="tpu_custom_call" | custom-call | tf_op jit(solution)/shard_map/pallas_call | solution.py:276
  13.5 18.9 %all-to-all-start = ((bf16[48,16,256]{2,1,0:T(8,128)(2,1)}), bf16[48,16,256]{2,1,0:T(8,128)(2,1)S(1)}, u32[]{:S(2)}, u32[]{:S(2)}) async-start(bf16[48,16,256]{2,1,0:T(8,128)(2,1)} %shard_map.55), calls=%async_computation | async-start | bytes 786432 | tf_op jit(solution)/shard_map/all_to_all | solution.py:284
  33.0 0.7 compare_select_fusion
  33.7 20.2 %all-to-all-done.refs_0_ = bf16[48,16,256]{2,1,0:T(8,128)(2,1)S(1)} async-done(((bf16[48,16,256]{2,1,0:T(8,128)(2,1)}), bf16[48,16,256]{2,1,0:T(8,128)(2,1)S(1)}, u32[]{:S(2)}, u32[]{:S(2)}) %all-to-all-start) | async-done | bytes 393248 | tf_op jit(solution)/shard_map/all_to_all | solution.py:284
  53.9 3.3 %shard_map.57 = (f32[24,2,16,128]{3,2,1,0:T(8,128)S(1)}, f32[24,2,16,128]{3,2,1,0:T(8,128)S(1)}) custom-call(s32[1]{0:T(128)} %copy.6.meta, s32[128]{0:T(128)S(1)} %get-tuple-element.11.sources, s32[128]{0:T(128)S(1)} %get-tuple-element.10.targets, bf16[48,16,256]{2,1,0:T(8,128)(2,1)S(1)} %all-to-all-done.refs_0_, bf16[128,128,128]{2,1,0:T(8,128)(2,1)} %refs_1_.1), custom_call_target="tpu_custom_call" | custom-call | tf_op jit(solution)/shard_map/pallas_call | solution.py:174
  57.3 1.9 %collective-permute-start.2 = (f32[24,2,16,128]{3,2,1,0:T(8,128)S(1)}, f32[24,2,16,128]{3,2,1,0:T(8,128)S(1)}, u32[]{:S(2)}, u32[]{:S(2)}) collective-permute-start(f32[24,2,16,128]{3,2,1,0:T(8,128)S(1)} %get-tuple-element.8), channel_id=1, source_target_pairs={{0,48},{48,0},{96,144},{144,96},{192,240},{240,192},{288,336},{336... | collective-permute-start | bytes 1179656 | tf_op jit(solution)/shard_map/ppermute | solution.py:307
  59.2 3.7 %collective-permute-start = (bf16[24,16,256]{2,1,0:T(8,128)(2,1)S(1)}, bf16[24,16,256]{2,1,0:T(8,128)(2,1)S(1)}, u32[]{:S(2)}, u32[]{:S(2)}) collective-permute-start(bf16[24,16,256]{2,1,0:T(8,128)(2,1)S(1)} %constant_dynamic-slice_fusion), channel_id=1, source_target_pairs={{0,384},{1,240},{2,192},{3,544},{4,208},{5,736},{6,128},{7,752},{8... | collective-permute-start | bytes 589832 | tf_op jit(solution)/shard_map/ppermute | solution.py:305
  63.0 0.0 collective-permute-done.2.came
  63.0 0.4 shard_map.58
  63.4 4.2 %collective-permute-start.3 = (s16[24,40,128]{2,1,0:T(8,128)(2,1)S(1)}, s16[24,40,128]{2,1,0:T(8,128)(2,1)S(1)}, u32[]{:S(2)}, u32[]{:S(2)}) collective-permute-start(s16[24,40,128]{2,1,0:T(8,128)(2,1)S(1)} %shard_map.58), channel_id=1, source_target_pairs={{384,0},{240,1},{192,2},{544,3},{208,4},{736,5},{128,6},{752,7},{7... | collective-permute-start | bytes 737288 | tf_op jit(solution)/shard_map/ppermute | solution.py:309
  67.7 7.2 %collective-permute-done.refs_0_ = bf16[24,16,256]{2,1,0:T(8,128)(2,1)S(1)} collective-permute-done((bf16[24,16,256]{2,1,0:T(8,128)(2,1)S(1)}, bf16[24,16,256]{2,1,0:T(8,128)(2,1)S(1)}, u32[]{:S(2)}, u32[]{:S(2)}) %collective-permute-start) | collective-permute-done | bytes 196640 | tf_op jit(solution)/shard_map/ppermute | solution.py:305
  74.9 1.9 %collective-permute-start.1 = (bf16[24,16,256]{2,1,0:T(8,128)(2,1)S(1)}, bf16[24,16,256]{2,1,0:T(8,128)(2,1)S(1)}, u32[]{:S(2)}, u32[]{:S(2)}) collective-permute-start(bf16[24,16,256]{2,1,0:T(8,128)(2,1)S(1)} %collective-permute-done.refs_0_), channel_id=1, source_target_pairs={{0,48},{48,0},{96,144},{144,96},{192,240},{240,192},{288,336},{336... | collective-permute-start | bytes 589832 | tf_op jit(solution)/shard_map/ppermute | solution.py:311
  76.8 1.4 %collective-permute-done.1.refs_1_ = bf16[24,16,256]{2,1,0:T(8,128)(2,1)S(1)} collective-permute-done((bf16[24,16,256]{2,1,0:T(8,128)(2,1)S(1)}, bf16[24,16,256]{2,1,0:T(8,128)(2,1)S(1)}, u32[]{:S(2)}, u32[]{:S(2)}) %collective-permute-start.1) | collective-permute-done | bytes 196640 | tf_op jit(solution)/shard_map/ppermute | solution.py:311
  78.2 0.0 copy-done.1
  78.2 0.0 copy-start
  78.2 2.2 %copy-done = bf16[128,128,128]{2,1,0:T(8,128)(2,1)S(1)} copy-done((bf16[128,128,128]{2,1,0:T(8,128)(2,1)S(1)}, bf16[128,128,128]{2,1,0:T(8,128)(2,1)}, u32[]{:S(2)}) %copy-start) | copy-done | bytes 4194328
  80.4 3.0 %shard_map.56.sums = f32[48,2,16,128]{3,2,1,0:T(8,128)S(1)} custom-call(s32[1]{0:T(128)} %copy.6.meta, s32[128]{0:T(128)S(1)} %get-tuple-element.9.sources, s32[128]{0:T(128)S(1)} %copy-done.1, bf16[24,16,256]{2,1,0:T(8,128)(2,1)S(1)} %collective-permute-done.refs_0_, bf16[24,16,256]{2,1,0:T(8,128)(2,1)S(1)} %collective-permute-done.1.refs_1_, ...), custom_call_target="tpu_custom_call" | custom-call | tf_op jit(solution)/shard_map/pallas_call | solution.py:174
  83.4 0.0 collective-permute-done.3.came
  83.4 0.9 shard_map.59
  84.3 44.9 %all_to_all.10.payload = s16[48,40,128]{2,1,0:T(8,128)(2,1)S(1)} all-to-all(s16[48,40,128]{2,1,0:T(8,128)(2,1)S(1)} %shard_map.59), channel_id=1, replica_groups=mesh['row'=16,'col'=48] {'col'}, dimensions={0} | all-to-all | bytes 983040 | tf_op jit(solution)/shard_map/all_to_all | solution.py:314
  129.2 1.3 %shard_map.60 = f32[16,256]{1,0:T(8,128)} custom-call(s16[48,40,128]{2,1,0:T(8,128)(2,1)S(1)} %all_to_all.10.payload), custom_call_target="tpu_custom_call" | custom-call | tf_op jit(solution)/shard_map/pallas_call | solution.py:244
  (1 shorter events, 0.0 us)
Async XLA Ops:
  0.0 78.2 %copy-start.1 = (s32[128]{0:T(128)S(1)}, s32[128]{0:T(128)}, u32[]{:S(2)}) copy-start(s32[128]{0:T(128)} %targets.1) | copy-start | bytes 1540
  13.5 40.5 %all-to-all-start = ((bf16[48,16,256]{2,1,0:T(8,128)(2,1)}), bf16[48,16,256]{2,1,0:T(8,128)(2,1)S(1)}, u32[]{:S(2)}, u32[]{:S(2)}) async-start(bf16[48,16,256]{2,1,0:T(8,128)(2,1)} %shard_map.55), calls=%async_computation | async-start | bytes 786432 | tf_op jit(solution)/shard_map/all_to_all | solution.py:284
  57.3 5.7 %collective-permute-start.2 = (f32[24,2,16,128]{3,2,1,0:T(8,128)S(1)}, f32[24,2,16,128]{3,2,1,0:T(8,128)S(1)}, u32[]{:S(2)}, u32[]{:S(2)}) collective-permute-start(f32[24,2,16,128]{3,2,1,0:T(8,128)S(1)} %get-tuple-element.8), channel_id=1, source_target_pairs={{0,48},{48,0},{96,144},{144,96},{192,240},{240,192},{288,336},{336... | collective-permute-start | bytes 1179656 | tf_op jit(solution)/shard_map/ppermute | solution.py:307
  59.2 15.7 %collective-permute-start = (bf16[24,16,256]{2,1,0:T(8,128)(2,1)S(1)}, bf16[24,16,256]{2,1,0:T(8,128)(2,1)S(1)}, u32[]{:S(2)}, u32[]{:S(2)}) collective-permute-start(bf16[24,16,256]{2,1,0:T(8,128)(2,1)S(1)} %constant_dynamic-slice_fusion), channel_id=1, source_target_pairs={{0,384},{1,240},{2,192},{3,544},{4,208},{5,736},{6,128},{7,752},{8... | collective-permute-start | bytes 589832 | tf_op jit(solution)/shard_map/ppermute | solution.py:305
  63.4 20.0 %collective-permute-start.3 = (s16[24,40,128]{2,1,0:T(8,128)(2,1)S(1)}, s16[24,40,128]{2,1,0:T(8,128)(2,1)S(1)}, u32[]{:S(2)}, u32[]{:S(2)}) collective-permute-start(s16[24,40,128]{2,1,0:T(8,128)(2,1)S(1)} %shard_map.58), channel_id=1, source_target_pairs={{384,0},{240,1},{192,2},{544,3},{208,4},{736,5},{128,6},{752,7},{7... | collective-permute-start | bytes 737288 | tf_op jit(solution)/shard_map/ppermute | solution.py:309
  74.9 3.3 %collective-permute-start.1 = (bf16[24,16,256]{2,1,0:T(8,128)(2,1)S(1)}, bf16[24,16,256]{2,1,0:T(8,128)(2,1)S(1)}, u32[]{:S(2)}, u32[]{:S(2)}) collective-permute-start(bf16[24,16,256]{2,1,0:T(8,128)(2,1)S(1)} %collective-permute-done.refs_0_), channel_id=1, source_target_pairs={{0,48},{48,0},{96,144},{144,96},{192,240},{240,192},{288,336},{336... | collective-permute-start | bytes 589832 | tf_op jit(solution)/shard_map/ppermute | solution.py:311
  78.2 2.2 %copy-start = (bf16[128,128,128]{2,1,0:T(8,128)(2,1)S(1)}, bf16[128,128,128]{2,1,0:T(8,128)(2,1)}, u32[]{:S(2)}) copy-start(bf16[128,128,128]{2,1,0:T(8,128)(2,1)} %refs_1_.1) | copy-start | bytes 12582916
where the time goes:
time: 131 us
  blocking collectives  44.9 us (34%)
  starting transfers between devices  30.7 us (23%)
  waiting for transfers between devices  28.9 us (22%)
  Pallas kernels  22.4 us (17%)
  local copies, waits for them, and re-layouts  2.21 us (2%)
    all_to_all x1, blocking collectives, shards(): plain = lax.all_to_all(plain, 'col', 0, 0, tiled=True)  44.9 us
    all_to_all x1, waiting for transfers between devices, spread(): return lax.all_to_all(copies, axes, 0, 0, tiled=True)  20.2 us
    all_to_all x1, starting transfers between devices, spread(): return lax.all_to_all(copies, axes, 0, 0, tiled=True)  18.9 us
    pallas_call x1, Pallas kernels, spread(): pl.pallas_call(copies_kernel, out_shape=jax.ShapeDtypeStruct((size, *arra...  13.5 us
    ppermute x1, waiting for transfers between devices, shards(): mine = lax.ppermute(mine, axes, out)  7.25 us
    pallas_call x2, Pallas kernels, products(): pl.pallas_call(functools.partial(product_kernel, mirror), out_shape=shape...  6.29 us
    ppermute x1, starting transfers between devices, shards(): sums = lax.ppermute(sums, axes, back)  4.22 us
    ppermute x1, starting transfers between devices, shards(): mine = lax.ppermute(mine, axes, out)  3.73 us
  transfers between devices with their start and end apart: 5, of which 3 were waited for; matrix products, arithmetic and copies ran while one was open for 1% of the time, Pallas kernels for 3%

commit v1 on v0

--- a/solution.py
+++ b/solution.py
@@ -260,28 +260,32 @@
     return pairs
 
 
-def copies_kernel(array, out, sems):
-    copies = [
-        pltpu.make_async_copy(array, out.at[i], sems.at[i]) for i in range(out.shape[0])
-    ]
-    for copy in copies:
-        copy.start()
-    for copy in copies:
-        copy.wait()
+def copies_kernel(array, out, held, sem):
+    copy = pltpu.make_async_copy(array, held, sem)
+    copy.start()
+    copy.wait()
+    out[...] = jnp.broadcast_to(held[...][None], out.shape)
 
 
 def spread(array, axes):
     size = lax.axis_size(axes)
-    hbm = pl.BlockSpec(memory_space=pltpu.HBM)
-    copies = pl.pallas_call(
-        copies_kernel,
-        out_shape=jax.ShapeDtypeStruct((size, *array.shape), array.dtype),
-        in_specs=[hbm],
-        out_specs=hbm,
-        scratch_shapes=[pltpu.SemaphoreType.DMA((size,))],
-        compiler_params=grant(2),
-    )(pltpu.with_memory_space_constraint(array, pltpu.HBM))
-    return lax.all_to_all(copies, axes, 0, 0, tiled=True)
+    return lax.all_to_all(
+        pl.pallas_call(
+            copies_kernel,
+            out_shape=jax.ShapeDtypeStruct((size, *array.shape), array.dtype),
+            in_specs=[pl.BlockSpec(memory_space=pltpu.HBM)],
+            out_specs=vmem(),
+            scratch_shapes=[
+                pltpu.VMEM(array.shape, array.dtype),
+                pltpu.SemaphoreType.DMA,
+            ],
+            compiler_params=grant(2),
+        )(pltpu.with_memory_space_constraint(array, pltpu.HBM)),
+        axes,
+        0,
+        0,
+        tiled=True,
+    )
 
 
 def shards(out, back, vectors, tiles, tile_rows, tile_cols, tile_count):

time: 131 us -> 119 us (0.908)
  Pallas kernels: 22.4 us -> 10.4 us
    pallas_call x1, Pallas kernels: 13.5 us -> 1.48 us  [spread(): pl.pallas_call(copies_kernel, out_shape=jax.ShapeDtypeStruct((size, *arra...]
where the time goes in v1:
time: 119 us
  blocking collectives  44.9 us (38%)
  starting transfers between devices  30.7 us (26%)
  waiting for transfers between devices  28.9 us (24%)
  Pallas kernels  10.4 us (9%)
  local copies, waits for them, and re-layouts  2.21 us (2%)
    all_to_all x1, blocking collectives, shards(): plain = lax.all_to_all(plain, 'col', 0, 0, tiled=True)  44.9 us
    all_to_all x1, waiting for transfers between devices, spread(): lax.all_to_all(pl.pallas_call(copies_kernel, out_shape=jax.ShapeDtypeStru...  20.2 us
    all_to_all x1, starting transfers between devices, spread(): lax.all_to_all(pl.pallas_call(copies_kernel, out_shape=jax.ShapeDtypeStru...  18.9 us
    ppermute x1, waiting for transfers between devices, shards(): mine = lax.ppermute(mine, axes, out)  7.25 us
    pallas_call x2, Pallas kernels, products(): pl.pallas_call(functools.partial(product_kernel, mirror), out_shape=shape...  6.29 us
    ppermute x1, starting transfers between devices, shards(): sums = lax.ppermute(sums, axes, back)  4.22 us
    ppermute x1, starting transfers between devices, shards(): mine = lax.ppermute(mine, axes, out)  3.73 us
  transfers between devices with their start and end apart: 5, of which 3 were waited for; matrix products, arithmetic and copies ran while one was open for 1% of the time, Pallas kernels for 3%

profile of v1, /device:TPU:6, one launch (start us, length us, event | category | flops | bytes accessed | tf_op | source)
XLA Modules:
  0.0 118.6 jit_solution(9049517861785605644)
XLA Ops:
  0.0 0.0 copy-start.1
  0.0 1.5 %shard_map.55 = bf16[48,16,256]{2,1,0:T(8,128)(2,1)} custom-call(bf16[16,256]{1,0:T(8,128)(2,1)} %array.1), custom_call_target="tpu_custom_call" | custom-call | tf_op jit(solution)/shard_map/pallas_call | solution.py:273
  1.5 18.9 %all-to-all-start = ((bf16[48,16,256]{2,1,0:T(8,128)(2,1)}), bf16[48,16,256]{2,1,0:T(8,128)(2,1)S(1)}, u32[]{:S(2)}, u32[]{:S(2)}) async-start(bf16[48,16,256]{2,1,0:T(8,128)(2,1)} %shard_map.55), calls=%async_computation | async-start | bytes 786432 | tf_op jit(solution)/shard_map/all_to_all | solution.py:272
  21.1 0.7 compare_select_fusion
  21.8 20.2 %all-to-all-done.refs_0_ = bf16[48,16,256]{2,1,0:T(8,128)(2,1)S(1)} async-done(((bf16[48,16,256]{2,1,0:T(8,128)(2,1)}), bf16[48,16,256]{2,1,0:T(8,128)(2,1)S(1)}, u32[]{:S(2)}, u32[]{:S(2)}) %all-to-all-start) | async-done | bytes 393248 | tf_op jit(solution)/shard_map/all_to_all | solution.py:272
  42.0 3.3 %shard_map.57 = (f32[24,2,16,128]{3,2,1,0:T(8,128)S(1)}, f32[24,2,16,128]{3,2,1,0:T(8,128)S(1)}) custom-call(s32[1]{0:T(128)} %copy.6.meta, s32[128]{0:T(128)S(1)} %get-tuple-element.11.sources, s32[128]{0:T(128)S(1)} %get-tuple-element.10.targets, bf16[48,16,256]{2,1,0:T(8,128)(2,1)S(1)} %all-to-all-done.refs_0_, bf16[128,128,128]{2,1,0:T(8,128)(2,1)} %refs_1_.1), custom_call_target="tpu_custom_call" | custom-call | tf_op jit(solution)/shard_map/pallas_call | solution.py:174
  45.3 1.9 %collective-permute-start.2 = (f32[24,2,16,128]{3,2,1,0:T(8,128)S(1)}, f32[24,2,16,128]{3,2,1,0:T(8,128)S(1)}, u32[]{:S(2)}, u32[]{:S(2)}) collective-permute-start(f32[24,2,16,128]{3,2,1,0:T(8,128)S(1)} %get-tuple-element.8), channel_id=1, source_target_pairs={{0,48},{48,0},{96,144},{144,96},{192,240},{240,192},{288,336},{336... | collective-permute-start | bytes 1179656 | tf_op jit(solution)/shard_map/ppermute | solution.py:311
  47.3 3.7 %collective-permute-start = (bf16[24,16,256]{2,1,0:T(8,128)(2,1)S(1)}, bf16[24,16,256]{2,1,0:T(8,128)(2,1)S(1)}, u32[]{:S(2)}, u32[]{:S(2)}) collective-permute-start(bf16[24,16,256]{2,1,0:T(8,128)(2,1)S(1)} %constant_dynamic-slice_fusion), channel_id=1, source_target_pairs={{0,384},{1,240},{2,192},{3,544},{4,208},{5,736},{6,128},{7,752},{8... | collective-permute-start | bytes 589832 | tf_op jit(solution)/shard_map/ppermute | solution.py:309
  51.0 0.0 collective-permute-done.2.came
  51.0 0.4 shard_map.58
  51.4 4.2 %collective-permute-start.3 = (s16[24,40,128]{2,1,0:T(8,128)(2,1)S(1)}, s16[24,40,128]{2,1,0:T(8,128)(2,1)S(1)}, u32[]{:S(2)}, u32[]{:S(2)}) collective-permute-start(s16[24,40,128]{2,1,0:T(8,128)(2,1)S(1)} %shard_map.58), channel_id=1, source_target_pairs={{384,0},{240,1},{192,2},{544,3},{208,4},{736,5},{128,6},{752,7},{7... | collective-permute-start | bytes 737288 | tf_op jit(solution)/shard_map/ppermute | solution.py:313
  55.7 7.2 %collective-permute-done.refs_0_ = bf16[24,16,256]{2,1,0:T(8,128)(2,1)S(1)} collective-permute-done((bf16[24,16,256]{2,1,0:T(8,128)(2,1)S(1)}, bf16[24,16,256]{2,1,0:T(8,128)(2,1)S(1)}, u32[]{:S(2)}, u32[]{:S(2)}) %collective-permute-start) | collective-permute-done | bytes 196640 | tf_op jit(solution)/shard_map/ppermute | solution.py:309
  62.9 1.9 %collective-permute-start.1 = (bf16[24,16,256]{2,1,0:T(8,128)(2,1)S(1)}, bf16[24,16,256]{2,1,0:T(8,128)(2,1)S(1)}, u32[]{:S(2)}, u32[]{:S(2)}) collective-permute-start(bf16[24,16,256]{2,1,0:T(8,128)(2,1)S(1)} %collective-permute-done.refs_0_), channel_id=1, source_target_pairs={{0,48},{48,0},{96,144},{144,96},{192,240},{240,192},{288,336},{336... | collective-permute-start | bytes 589832 | tf_op jit(solution)/shard_map/ppermute | solution.py:315
  64.8 1.4 %collective-permute-done.1.refs_1_ = bf16[24,16,256]{2,1,0:T(8,128)(2,1)S(1)} collective-permute-done((bf16[24,16,256]{2,1,0:T(8,128)(2,1)S(1)}, bf16[24,16,256]{2,1,0:T(8,128)(2,1)S(1)}, u32[]{:S(2)}, u32[]{:S(2)}) %collective-permute-start.1) | collective-permute-done | bytes 196640 | tf_op jit(solution)/shard_map/ppermute | solution.py:315
  66.2 0.0 copy-done.1
  66.3 0.0 copy-start
  66.3 2.2 %copy-done = bf16[128,128,128]{2,1,0:T(8,128)(2,1)S(1)} copy-done((bf16[128,128,128]{2,1,0:T(8,128)(2,1)S(1)}, bf16[128,128,128]{2,1,0:T(8,128)(2,1)}, u32[]{:S(2)}) %copy-start) | copy-done | bytes 4194328
  68.4 3.0 %shard_map.56.sums = f32[48,2,16,128]{3,2,1,0:T(8,128)S(1)} custom-call(s32[1]{0:T(128)} %copy.6.meta, s32[128]{0:T(128)S(1)} %get-tuple-element.9.sources, s32[128]{0:T(128)S(1)} %copy-done.1, bf16[24,16,256]{2,1,0:T(8,128)(2,1)S(1)} %collective-permute-done.refs_0_, bf16[24,16,256]{2,1,0:T(8,128)(2,1)S(1)} %collective-permute-done.1.refs_1_, ...), custom_call_target="tpu_custom_call" | custom-call | tf_op jit(solution)/shard_map/pallas_call | solution.py:174
  71.4 0.0 collective-permute-done.3.came
  71.4 0.9 shard_map.59
  72.3 44.9 %all_to_all.10.payload = s16[48,40,128]{2,1,0:T(8,128)(2,1)S(1)} all-to-all(s16[48,40,128]{2,1,0:T(8,128)(2,1)S(1)} %shard_map.59), channel_id=1, replica_groups=mesh['row'=16,'col'=48] {'col'}, dimensions={0} | all-to-all | bytes 983040 | tf_op jit(solution)/shard_map/all_to_all | solution.py:318
  117.2 1.3 %shard_map.60 = f32[16,256]{1,0:T(8,128)} custom-call(s16[48,40,128]{2,1,0:T(8,128)(2,1)S(1)} %all_to_all.10.payload), custom_call_target="tpu_custom_call" | custom-call | tf_op jit(solution)/shard_map/pallas_call | solution.py:244
  (1 shorter events, 0.0 us)
Async XLA Ops:
  0.0 66.3 %copy-start.1 = (s32[128]{0:T(128)S(1)}, s32[128]{0:T(128)}, u32[]{:S(2)}) copy-start(s32[128]{0:T(128)} %targets.1) | copy-start | bytes 1540
  1.5 40.5 %all-to-all-start = ((bf16[48,16,256]{2,1,0:T(8,128)(2,1)}), bf16[48,16,256]{2,1,0:T(8,128)(2,1)S(1)}, u32[]{:S(2)}, u32[]{:S(2)}) async-start(bf16[48,16,256]{2,1,0:T(8,128)(2,1)} %shard_map.55), calls=%async_computation | async-start | bytes 786432 | tf_op jit(solution)/shard_map/all_to_all | solution.py:272
  45.3 5.7 %collective-permute-start.2 = (f32[24,2,16,128]{3,2,1,0:T(8,128)S(1)}, f32[24,2,16,128]{3,2,1,0:T(8,128)S(1)}, u32[]{:S(2)}, u32[]{:S(2)}) collective-permute-start(f32[24,2,16,128]{3,2,1,0:T(8,128)S(1)} %get-tuple-element.8), channel_id=1, source_target_pairs={{0,48},{48,0},{96,144},{144,96},{192,240},{240,192},{288,336},{336... | collective-permute-start | bytes 1179656 | tf_op jit(solution)/shard_map/ppermute | solution.py:311
  47.3 15.7 %collective-permute-start = (bf16[24,16,256]{2,1,0:T(8,128)(2,1)S(1)}, bf16[24,16,256]{2,1,0:T(8,128)(2,1)S(1)}, u32[]{:S(2)}, u32[]{:S(2)}) collective-permute-start(bf16[24,16,256]{2,1,0:T(8,128)(2,1)S(1)} %constant_dynamic-slice_fusion), channel_id=1, source_target_pairs={{0,384},{1,240},{2,192},{3,544},{4,208},{5,736},{6,128},{7,752},{8... | collective-permute-start | bytes 589832 | tf_op jit(solution)/shard_map/ppermute | solution.py:309
  51.4 20.0 %collective-permute-start.3 = (s16[24,40,128]{2,1,0:T(8,128)(2,1)S(1)}, s16[24,40,128]{2,1,0:T(8,128)(2,1)S(1)}, u32[]{:S(2)}, u32[]{:S(2)}) collective-permute-start(s16[24,40,128]{2,1,0:T(8,128)(2,1)S(1)} %shard_map.58), channel_id=1, source_target_pairs={{384,0},{240,1},{192,2},{544,3},{208,4},{736,5},{128,6},{752,7},{7... | collective-permute-start | bytes 737288 | tf_op jit(solution)/shard_map/ppermute | solution.py:313
  62.9 3.3 %collective-permute-start.1 = (bf16[24,16,256]{2,1,0:T(8,128)(2,1)S(1)}, bf16[24,16,256]{2,1,0:T(8,128)(2,1)S(1)}, u32[]{:S(2)}, u32[]{:S(2)}) collective-permute-start(bf16[24,16,256]{2,1,0:T(8,128)(2,1)S(1)} %collective-permute-done.refs_0_), channel_id=1, source_target_pairs={{0,48},{48,0},{96,144},{144,96},{192,240},{240,192},{288,336},{336... | collective-permute-start | bytes 589832 | tf_op jit(solution)/shard_map/ppermute | solution.py:315
  66.3 2.2 %copy-start = (bf16[128,128,128]{2,1,0:T(8,128)(2,1)S(1)}, bf16[128,128,128]{2,1,0:T(8,128)(2,1)}, u32[]{:S(2)}) copy-start(bf16[128,128,128]{2,1,0:T(8,128)(2,1)} %refs_1_.1) | copy-start | bytes 12582916
